TPU v7x, 512 devices: a whole 4x8x8 slice. The times are simulated.
512 devices in a mesh: tile: 64 (over y, x, core), view: 8 (over z).
Axes of the slice: x: 4, y: 8, z: 8, core: 2. Of those that a mesh axis runs over, the one named last changes fastest.
Arguments:
- volume: float32 [64, 512, 512], P(None, 'tile'), may hold values from 0.09 to 7.2
- weights: bfloat16 [64, 32, 32, 48, 256], P('tile', 'view'), may hold values from 0 to 0.0546875
- measured: float32 [64, 8, 1, 64, 48], P('tile', 'view'), may hold values from 4 to 40
- crossings: int32 [64, 32, 32, 2], P('tile', 'view'), may hold values from 0 to 15, as said below
- counts: int32 [64, 32], P('tile', 'view'), may hold values from 16 to 32
Outputs:
- updated: float32 [64, 512, 512], P(None, 'tile')
Inputs may be any that keep to these rules, and one draw needn't show every extreme that they name: `crossings`: slots follow a parallel-beam geometry: each segment of a strip has one or two live slots, naming the one or two adjacent blocks that its pixels' footprints reach in that view; the live slots of a strip and view come first; a dead slot repeats the first block of its segment.
All inputs are finite; a program needn't handle non-finite values.
Results may differ from a plain program's by a relative error of at most 0.002.
Values may be sent and summed in bfloat16 or wider, within the bound.
A program may use at most 64 MiB of HBM per device.

v0:
```python
import jax
import jax.numpy as jnp
from jax import lax
from jax.sharding import PartitionSpec as P

BACKGROUND = 1.0
HUBER_DELTA = 0.1


def extended(x, sides, width):
    for axis, dim in sides:
        peers, length = (lax.axis_size(axis), x.shape[dim])
        up = [(i, (i + 1) % peers) for i in range(peers - 1)]
        down = [(j, i) for i, j in up]
        last = lax.slice_in_dim(x, length - width, length, axis=dim)
        initial = lax.slice_in_dim(x, 0, width, axis=dim)
        before = lax.ppermute(last, axis, up)
        after = lax.ppermute(initial, axis, down)
        x = jnp.concatenate([before, x, after], axis=dim)
    return x


def per_device(volume, weights, measured, crossings, counts):
    high = lax.Precision.HIGHEST
    tile_count = lax.axis_size("tile")
    view_local = weights.shape[1]
    slot_count = weights.shape[2]
    bin_count = weights.shape[3]
    seg_pixels = weights.shape[4]
    plane_count = volume.shape[0]
    row_count = volume.shape[1]
    col_count = volume.shape[2]
    seg_cols = seg_pixels // row_count
    seg_total = col_count // seg_cols
    owned = measured.shape[2]
    blocks_view = owned * tile_count // view_local
    block_total = tile_count * owned
    slot_total = view_local * slot_count
    flat_width = plane_count * bin_count
    slot_weights = weights.reshape(slot_total, bin_count, seg_pixels)
    block_of = crossings[0, :, :, 0].reshape(slot_total)
    segment_of = crossings[0, :, :, 1].reshape(slot_total)
    alive = (jnp.arange(slot_count, dtype=jnp.int32)[None, :] < counts[0][:, None]).reshape(
        slot_total
    )
    alive_f = alive.astype(jnp.float32)
    view_slot = jnp.arange(slot_total, dtype=jnp.int32) // slot_count
    global_block = view_slot * blocks_view + block_of
    block_onehot = (
        global_block[:, None] == jnp.arange(block_total, dtype=jnp.int32)[None, :]
    ).astype(jnp.float32)
    block_onehot = block_onehot * alive_f[:, None]
    segment_onehot = (
        segment_of[:, None] == jnp.arange(seg_total, dtype=jnp.int32)[None, :]
    ).astype(jnp.float32)
    segments = volume.astype(jnp.bfloat16).reshape(plane_count, row_count, seg_total, seg_cols)
    segments = segments.transpose(0, 2, 1, 3).reshape(plane_count, seg_total, seg_pixels)
    slot_volume = jnp.einsum(
        "sq,pqx->spx",
        segment_onehot.astype(jnp.bfloat16),
        segments,
        preferred_element_type=jnp.float32,
    ).astype(jnp.bfloat16)
    partial_value = jnp.einsum(
        "spx,snx->spn", slot_volume, slot_weights, preferred_element_type=jnp.float32
    )
    dense = jnp.dot(block_onehot.T, partial_value.reshape(slot_total, flat_width), precision=high)
    dense = dense.reshape(tile_count, owned, flat_width)
    projection = lax.psum_scatter(dense, "tile", scatter_dimension=0, tiled=True)[0]
    ratios = (measured[0, 0].reshape(owned, flat_width) / (projection + BACKGROUND)).astype(
        jnp.bfloat16
    )
    every_block = lax.all_gather(ratios, "tile", axis=0, tiled=True)
    picked = jnp.dot(
        block_onehot.astype(jnp.bfloat16), every_block, preferred_element_type=jnp.float32
    ).astype(jnp.bfloat16)
    picked = picked.reshape(slot_total, plane_count, bin_count)
    spread_back = jnp.einsum(
        "spn,snx->spx", picked, slot_weights, preferred_element_type=jnp.float32
    )
    back_sum = jnp.einsum("sq,spx->pqx", segment_onehot, spread_back, precision=high)
    back_sum = back_sum.reshape(plane_count, seg_total, row_count, seg_cols).transpose(0, 2, 1, 3)
    back_sum = back_sum.reshape(volume.shape)
    live_segments = (segment_onehot * alive_f[:, None]).astype(jnp.bfloat16)
    sensitivity = jnp.einsum(
        "sq,snx->qx", live_segments, slot_weights, preferred_element_type=jnp.float32
    )
    sensitivity = (
        sensitivity.reshape(seg_total, row_count, seg_cols)
        .transpose(1, 0, 2)
        .reshape(row_count, col_count)
    )
    widened = extended(volume, (("tile", 1),), 1)
    padded = jnp.pad(widened, ((1, 1), (0, 0), (1, 1)))
    centre = padded[1:-1, 1:-1, 1:-1]
    penalty = jnp.zeros_like(volume)
    for other in (
        padded[2:, 1:-1, 1:-1],
        padded[:-2, 1:-1, 1:-1],
        padded[1:-1, 2:, 1:-1],
        padded[1:-1, :-2, 1:-1],
        padded[1:-1, 1:-1, 2:],
        padded[1:-1, 1:-1, :-2],
    ):
        penalty = penalty + jnp.clip(centre - other, -HUBER_DELTA, HUBER_DELTA)
    back_total, sens_total = lax.psum((back_sum, sensitivity), "view")
    return volume * back_total / (sens_total[None] * (1.0 + penalty))


def solution(mesh):
    in_specs = (
        P(None, "tile", None),
        P("tile", "view", None, None, None),
        P("tile", "view", None, None, None),
        P("tile", "view", None, None),
        P("tile", "view"),
    )
    out_specs = P(None, "tile", None)
    return jax.shard_map(
        per_device, mesh=mesh, in_specs=in_specs, out_specs=out_specs, check_vma=False
    )
```

profile of v0, /device:TPU:2, one launch (start us, length us, event | category | flops | bytes accessed | tf_op | source)
XLA Modules:
  0.0 397.6 jit_solution(3167328225006800716)
XLA Ops:
  6.5 0.0 all-reduce.7.cloned.1.call-start
  6.5 0.8 slice_reduce_fusion.1
  7.3 0.1 eq.31
  7.4 1.8 copy.79
  9.2 0.1 copy.80
  9.3 1.6 copy.81
  11.0 2.5 convolution_convert_fusion.1
  13.4 0.0 copy-done
  13.4 4.5 %fusion.2 = f32[128,64,48]{1,2,0:T(8,128)} fusion(bf16[128,48,256]{2,1,0:T(8,128)(2,1)S(1)} %bitcast.51, bf16[128,64,256]{2,0,1:T(8,128)(2,1)S(1)} %convolution_convert_fusion.1), kind=kOutput, calls=%fused_computation.3 | convolution fusion | flops 201326592 | bytes 8912896 | tf_op jit(solution)/shard_map/spx,snx->spn/dot_general | solution.py:64
  17.9 0.0 copy-start.2
  17.9 3.3 copy.83
  21.2 0.0 copy-start.1
  21.2 0.1 reshape_squeeze.6
  21.3 0.0 copy-done.2
  21.3 0.1 fusion.48
  21.3 0.1 reshape.107
  21.4 4.1 %convolution_bitcast_fusion = f32[64,1,3072]{2,0,1:T(8,128)} fusion(f32[128,3072]{0,1:T(8,128)} %bitcast.55, f32[128]{0:T(128)S(1)} %reshape.107, s32[128]{0:T(128)S(1)} %fusion.50), kind=kOutput, calls=%fused_computation.10 | convolution fusion | flops 302006272 | bytes 2360320 | tf_op jit(solution)/shard_map/dot_general | solution.py:67
  25.5 0.0 all-reduce.7.cloned.1.call-update
  25.6 0.0 all-reduce.5.cloned.1.call-start
  25.6 0.0 copy-done.1
  25.6 0.1 copy.78
  25.7 0.1 reshape_squeeze.7
  25.8 1.3 dynamic-slice
  27.2 199.2 %all-reduce.7.cloned.1.call-done = f32[64,1,3072]{2,0,1:T(8,128)} async-done(((f32[64,1,3072]{2,0,1:T(8,128)}), f32[64,1,3072]{2,0,1:T(8,128)}) %all-reduce.7.cloned.1.call-update) | async-done | bytes 786448
  226.4 1.6 convert_bitcast_fusion
  227.9 48.3 %all-gather = bf16[64,1,3072]{2,1,0:T(2,128)(2,1)S(1)} all-gather(bf16[1,1,3072]{2,1,0:T(2,128)(2,1)S(1)} %convert_bitcast_fusion), channel_id=1, replica_groups=mesh['tile'=64,'view'=8] {'tile'}, dimensions={0}, use_global_device_ids=true | all-gather | bytes 399360 | tf_op jit(solution)/shard_map/all_gather | solution.py:73
  276.3 1.3 convolution_convert_fusion
  277.6 2.3 copy.84
  279.9 3.1 copy.85
  283.0 2.7 fusion.55
  285.7 8.5 %fusion.7 = f32[64,16,256]{2,1,0:T(8,128)} fusion(f32[128,64,256]{2,1,0:T(8,128)S(1)} %fusion.55, s32[128]{0:T(128)S(1)} %eq.31), kind=kOutput, calls=%fused_computation.17 | convolution fusion | flops 402655232 | bytes 9437696 | tf_op jit(solution)/shard_map/sq,spx->pqx/dot_general | solution.py:81
  294.2 3.2 copy.87
  297.4 3.1 copy.88
  300.5 3.4 copy.89
  303.9 0.0 all-reduce.5.cloned.1.call-update
  303.9 2.5 fusion.54
  306.4 2.3 collective-permute-start
  308.7 3.5 collective-permute-start.1
  312.2 0.9 convert_reduce_fusion
  313.1 0.1 copy.90
  313.2 0.2 convolution_bitcast_fusion.1
  313.4 0.1 reshape.106
  313.5 30.9 %psum.15 = f32[8,512]{1,0:T(8,128)S(1)} all-reduce(f32[8,512]{1,0:T(8,128)S(1)} %reshape.106), channel_id=1, replica_groups=mesh['tile'=64,'view'=8] {'view'}, use_global_device_ids=true, to_apply=%region_3.4 | all-reduce | flops 4096 | bytes 32768 | tf_op jit(solution)/shard_map/psum | solution.py:106
  344.3 0.0 collective-permute-done
  344.3 0.0 collective-permute-done.1
  344.3 3.0 select_maximum_fusion
  347.3 38.9 %all-reduce.5.cloned.1.call-done = f32[64,8,512]{2,1,0:T(8,128)} async-done(((f32[64,8,512]{2,1,0:T(8,128)}), f32[64,8,512]{2,1,0:T(8,128)}) %all-reduce.5.cloned.1.call-update) | async-done | bytes 1048592 | tf_op jit(solution)/shard_map/psum | solution.py:106
  386.2 4.5 %fusion.14 = f32[64,8,512]{2,1,0:T(8,128)} fusion(f32[64,8,512]{2,1,0:T(8,128)} %param.5, f32[66,10,514]{2,1,0:T(8,128)S(1)} %select_maximum_fusion, f32[64,1,512]{2,1,0:T(1,128)S(1)} %collective-permute-done, f32[64,1,512]{2,1,0:T(1,128)S(1)} %collective-permute-done.1, f32[64,8,512]{2,1,0:T(8,128)} %all-reduce.5.cloned.1.call-done, f32[8,512]{1,0:T(8,128)S(1)} %psum.15), kind=kLoop, calls=%fused_computation.24 | loop fusion | flops 6029312 | bytes 7618560 | tf_op jit(solution)/shard_map/div | solution.py:107
  (2 shorter events, 0.0 us)
Async XLA Ops:
  6.5 219.8 %all-reduce.7.cloned.1.call-start = ((), (), s32[]{:S(2)}) async-start(), calls=%async_computation.1 | async-start | bytes 1572864
  11.0 2.5 copy-start
  17.9 3.4 copy-start.2
  21.2 4.5 %copy-start.1 = (f32[1,1,1,64,48]{3,4,2,1,0:T(8,128)S(1)}, f32[1,1,1,64,48]{3,4,2,1,0:T(8,128)}, u32[]{:S(2)}) copy-start(f32[1,1,1,64,48]{3,4,2,1,0:T(8,128)} %param.7) | copy-start | bytes 36868
  25.6 360.7 %all-reduce.5.cloned.1.call-start = ((), (), s32[]{:S(2)}) async-start(), calls=%async_computation | async-start | bytes 2097152 | tf_op jit(solution)/shard_map/psum | solution.py:106
  306.4 38.0 %collective-permute-start = (f32[64,1,512]{2,1,0:T(1,128)}, f32[64,1,512]{2,1,0:T(1,128)S(1)}, u32[]{:S(2)}, u32[]{:S(2)}) collective-permute-start(f32[64,1,512]{2,1,0:T(1,128)} %get-tuple-element.7), channel_id=1, source_target_pairs={{0,8},{8,16},{16,24},{24,32},{32,40},{40,48},{48,56},{56,64},{64,7... | collective-permute-start | bytes 393224 | tf_op jit(solution)/shard_map/ppermute | solution.py:17
  308.7 35.7 %collective-permute-start.1 = (f32[64,1,512]{2,1,0:T(1,128)}, f32[64,1,512]{2,1,0:T(1,128)S(1)}, u32[]{:S(2)}, u32[]{:S(2)}) collective-permute-start(f32[64,1,512]{2,1,0:T(1,128)} %get-tuple-element.8), channel_id=1, source_target_pairs={{8,0},{16,8},{24,16},{32,24},{40,32},{48,40},{56,48},{64,56},{72,6... | collective-permute-start | bytes 393224 | tf_op jit(solution)/shard_map/ppermute | solution.py:18
Sparse Core Ops, SparseCore 0:
  25.7 200.6 all-reduce.6
  304.0 82.1 all-reduce.4
where the time goes:
time: 398 us
  waiting for transfers between devices  238 us (60%)
  blocking collectives  79.2 us (20%)
  local copies, waits for them, and re-layouts  27.2 us (7%)
  matrix products  23.7 us (6%)
  between operations  13.5 us (3%)
  other arithmetic  9.96 us (3%)
  starting transfers between devices  5.81 us (1%)
    unnamed x3, waiting for transfers between devices  199 us
    all_gather x1, blocking collectives, per_device(): every_block = lax.all_gather(ratios, 'tile', axis=0, tiled=True)  48.3 us
    psum x1, waiting for transfers between devices, per_device(): back_total, sens_total = lax.psum((back_sum, sensitivity), 'view')  38.9 us
    psum x1, blocking collectives, per_device(): back_total, sens_total = lax.psum((back_sum, sensitivity), 'view')  30.9 us
    dot_general x1, matrix products, per_device(): jnp.einsum('sq,spx->pqx', segment_onehot, spread_back, precision=high)  8.51 us
  transfers between devices with their start and end apart: 4, of which 2 were waited for; matrix products, arithmetic and copies ran while one was open for 2% of the time, Pallas kernels for 0%

commit v1 on v0

--- a/solution.py
+++ b/solution.py
@@ -70,7 +70,9 @@
     ratios = (measured[0, 0].reshape(owned, flat_width) / (projection + BACKGROUND)).astype(
         jnp.bfloat16
     )
-    every_block = lax.all_gather(ratios, "tile", axis=0, tiled=True)
+    every_block = jnp.concatenate(
+        lax.all_to_all(jnp.stack([ratios] * lax.axis_size("tile")), "tile", 0, 0), axis=0
+    )
     picked = jnp.dot(
         block_onehot.astype(jnp.bfloat16), every_block, preferred_element_type=jnp.float32
     ).astype(jnp.bfloat16)

time: 398 us -> 383 us (0.962)
  blocking collectives: 79.2 us -> 54 us
  local copies, waits for them, and re-layouts: 27.2 us -> 33.9 us
  other arithmetic: 9.96 us -> 14.8 us
    all_gather x1 -> x0, blocking collectives: 48.3 us -> none  [per_device(): every_block = lax.all_gather(ratios, 'tile', axis=0, tiled=True)]
    all_to_all x0 -> x1, blocking collectives: none -> 23.2 us  [per_device(): lax.all_to_all(jnp.stack([ratios] * lax.axis_size('tile')), 'tile', 0, 0)]
    unnamed x9 -> x11, local copies, waits for them, and re-layouts: 3.22 us -> 8.05 us
    another operation x0 -> x1, other arithmetic: none -> 4.66 us  [per_device(): jnp.stack([ratios] * lax.axis_size('tile'))]
where the time goes in v1:
time: 383 us; the launch traced here: 382 us
  waiting for transfers between devices  235 us (61%)
  blocking collectives  54 us (14%)
  local copies, waits for them, and re-layouts  33.9 us (9%)
  matrix products  24.8 us (6%)
  other arithmetic  14.8 us (4%)
  between operations  13.5 us (4%)
  starting transfers between devices  5.81 us (2%)
    unnamed x3, waiting for transfers between devices  199 us
    psum x1, waiting for transfers between devices, per_device(): back_total, sens_total = lax.psum((back_sum, sensitivity), 'view')  36.2 us
    psum x1, blocking collectives, per_device(): back_total, sens_total = lax.psum((back_sum, sensitivity), 'view')  30.9 us
    all_to_all x1, blocking collectives, per_device(): lax.all_to_all(jnp.stack([ratios] * lax.axis_size('tile')), 'tile', 0, 0)  23.2 us
    dot_general x1, matrix products, per_device(): jnp.einsum('sq,spx->pqx', segment_onehot, spread_back, precision=high)  8.51 us
    unnamed x11, local copies, waits for them, and re-layouts  8.05 us
  transfers between devices with their start and end apart: 4, of which 2 were waited for; matrix products, arithmetic and copies ran while one was open for 2% of the time, Pallas kernels for 0%

profile of v1, /device:TPU:2, one launch (start us, length us, event | category | flops | bytes accessed | tf_op | source)
XLA Modules:
  0.0 382.4 jit_solution(3134934610237096411)
XLA Ops:
  6.5 0.0 all-reduce.7.cloned.1.call-start
  6.5 0.8 slice_reduce_fusion.1
  7.3 0.1 eq.31
  7.4 1.8 copy.83
  9.2 0.1 copy.84
  9.3 1.6 copy.85
  11.0 2.5 convolution_convert_fusion.1
  13.4 4.5 %fusion.2 = f32[128,64,48]{1,2,0:T(8,128)} fusion(bf16[128,48,256]{2,1,0:T(8,128)(2,1)S(1)} %bitcast.51, bf16[128,64,256]{2,0,1:T(8,128)(2,1)S(1)} %convolution_convert_fusion.1), kind=kOutput, calls=%fused_computation.3 | convolution fusion | flops 201326592 | bytes 8912896 | tf_op jit(solution)/shard_map/spx,snx->spn/dot_general | solution.py:64
  17.9 3.3 copy.87
  21.2 0.1 reshape_squeeze.6
  21.3 0.1 fusion.48
  21.3 0.1 reshape.92
  21.4 4.1 %convolution_bitcast_fusion = f32[64,1,3072]{2,0,1:T(8,128)} fusion(f32[128,3072]{0,1:T(8,128)} %bitcast.55, f32[128]{0:T(128)S(1)} %reshape.92, s32[128]{0:T(128)S(1)} %fusion.50), kind=kOutput, calls=%fused_computation.10 | convolution fusion | flops 302006272 | bytes 2360320 | tf_op jit(solution)/shard_map/dot_general | solution.py:67
  25.5 0.0 all-reduce.7.cloned.1.call-update
  25.6 0.0 all-reduce.5.cloned.1.call-start
  25.6 0.1 copy.82
  25.7 0.1 reshape_squeeze.7
  25.8 1.3 dynamic-slice
  27.2 199.2 %all-reduce.7.cloned.1.call-done = f32[64,1,3072]{2,0,1:T(8,128)} async-done(((f32[64,1,3072]{2,0,1:T(8,128)}), f32[64,1,3072]{2,0,1:T(8,128)}) %all-reduce.7.cloned.1.call-update) | async-done | bytes 786448
  226.4 1.6 convert_reduce_fusion.1
  228.0 1.3 stack.5
  229.3 0.6 broadcast.92
  229.8 4.7 %reduce.11 = bf16[64,3072]{1,0:T(8,128)(2,1)} reduce(bf16[64,1,3072]{2,1,0:T(2,128)(2,1)} %stack.5, bf16[]{:T(256)} %broadcast.92), dimensions={1}, to_apply=%stack.5.reduce_sub_computation | reduce | bytes 786434 | tf_op jit(solution)/shard_map/stack | solution.py:74
  234.5 1.3 reshape.112
  235.8 23.2 %all_to_all.5 = bf16[64,2,1536]{2,1,0:T(2,128)(2,1)} all-to-all(bf16[64,2,1536]{2,1,0:T(2,128)(2,1)S(1)} %reshape.112), channel_id=1, replica_groups=mesh['tile'=64,'view'=8] {'tile'}, dimensions={0} | all-to-all | bytes 786432 | tf_op jit(solution)/shard_map/all_to_all | solution.py:74
  258.9 3.5 reshape.113
  262.5 2.4 convolution_convert_fusion
  264.9 2.3 copy.89
  267.2 3.1 copy.90
  270.3 2.7 fusion.55
  273.0 8.5 %fusion.7 = f32[64,16,256]{2,1,0:T(8,128)} fusion(f32[128,64,256]{2,1,0:T(8,128)S(1)} %fusion.55, s32[128]{0:T(128)S(1)} %eq.31), kind=kOutput, calls=%fused_computation.17 | convolution fusion | flops 402655232 | bytes 9437696 | tf_op jit(solution)/shard_map/sq,spx->pqx/dot_general | solution.py:83
  281.5 3.2 copy.92
  284.7 3.1 copy.93
  287.8 3.4 copy.94
  291.2 0.0 all-reduce.5.cloned.1.call-update
  291.2 2.5 fusion.54
  293.7 2.1 collective-permute-start
  295.8 3.7 collective-permute-start.1
  299.5 0.9 convert_reduce_fusion
  300.4 0.1 copy.95
  300.5 0.2 convolution_bitcast_fusion.1
  300.7 0.1 reshape.91
  300.8 30.9 %psum.15 = f32[8,512]{1,0:T(8,128)S(1)} all-reduce(f32[8,512]{1,0:T(8,128)S(1)} %reshape.91), channel_id=1, replica_groups=mesh['tile'=64,'view'=8] {'view'}, use_global_device_ids=true, to_apply=%region_3.4 | all-reduce | flops 4096 | bytes 32768 | tf_op jit(solution)/shard_map/psum | solution.py:108
  331.7 0.0 collective-permute-done
  331.7 0.0 collective-permute-done.1
  331.7 3.0 select_maximum_fusion
  334.7 36.2 %all-reduce.5.cloned.1.call-done = f32[64,8,512]{2,1,0:T(8,128)} async-done(((f32[64,8,512]{2,1,0:T(8,128)}), f32[64,8,512]{2,1,0:T(8,128)}) %all-reduce.5.cloned.1.call-update) | async-done | bytes 1048592 | tf_op jit(solution)/shard_map/psum | solution.py:108
  370.9 4.7 %fusion.14 = f32[64,8,512]{2,1,0:T(8,128)} fusion(f32[64,8,512]{2,1,0:T(8,128)} %param.5, f32[66,10,514]{2,1,0:T(8,128)S(1)} %select_maximum_fusion, f32[64,1,512]{2,1,0:T(1,128)S(1)} %collective-permute-done, f32[64,1,512]{2,1,0:T(1,128)S(1)} %collective-permute-done.1, f32[64,8,512]{2,1,0:T(8,128)} %all-reduce.5.cloned.1.call-done, f32[8,512]{1,0:T(8,128)S(1)} %psum.15), kind=kLoop, calls=%fused_computation.24 | loop fusion | flops 6029312 | bytes 7618560 | tf_op jit(solution)/shard_map/div | solution.py:109
  (7 shorter events, 0.0 us)
Async XLA Ops:
  6.5 219.8 %all-reduce.7.cloned.1.call-start = ((), (), s32[]{:S(2)}) async-start(), calls=%async_computation.2 | async-start | bytes 1572864
  11.0 2.5 copy-start
  17.9 3.4 copy-start.2
  21.2 4.5 %copy-start.1 = (f32[1,1,1,64,48]{3,4,2,1,0:T(8,128)S(1)}, f32[1,1,1,64,48]{3,4,2,1,0:T(8,128)}, u32[]{:S(2)}) copy-start(f32[1,1,1,64,48]{3,4,2,1,0:T(8,128)} %param.7) | copy-start | bytes 36868
  25.6 345.3 %all-reduce.5.cloned.1.call-start = ((), (), s32[]{:S(2)}) async-start(), calls=%async_computation.1 | async-start | bytes 2097152 | tf_op jit(solution)/shard_map/psum | solution.py:108
  293.7 38.0 %collective-permute-start = (f32[64,1,512]{2,1,0:T(1,128)}, f32[64,1,512]{2,1,0:T(1,128)S(1)}, u32[]{:S(2)}, u32[]{:S(2)}) collective-permute-start(f32[64,1,512]{2,1,0:T(1,128)} %get-tuple-element.7), channel_id=1, source_target_pairs={{0,8},{8,16},{16,24},{24,32},{32,40},{40,48},{48,56},{56,64},{64,7... | collective-permute-start | bytes 393224 | tf_op jit(solution)/shard_map/ppermute | solution.py:17
  295.8 35.9 %collective-permute-start.1 = (f32[64,1,512]{2,1,0:T(1,128)}, f32[64,1,512]{2,1,0:T(1,128)S(1)}, u32[]{:S(2)}, u32[]{:S(2)}) collective-permute-start(f32[64,1,512]{2,1,0:T(1,128)} %get-tuple-element.8), channel_id=1, source_target_pairs={{8,0},{16,8},{24,16},{32,24},{40,32},{48,40},{56,48},{64,56},{72,6... | collective-permute-start | bytes 393224 | tf_op jit(solution)/shard_map/ppermute | solution.py:18
Sparse Core Ops, SparseCore 0:
  25.7 200.6 all-reduce.6
  291.3 79.4 all-reduce.4
